TPU v7x, 32 devices: a whole 2x2x4 slice. The times are simulated.
32 devices in a mesh: st: 8 (over y, x, core), tm: 4 (over z).
Axes of the slice: x: 2, y: 2, z: 4, core: 2. Of those that a mesh axis runs over, the one named last changes fastest.
Arguments:
- observed: float32 [8192, 2048], P('st', 'tm'), may hold values from -24 to 24
- station_xy: float32 [2, 8192], P(None, 'st'), may hold values from 0 to 33
- site_xy: float32 [2, 4096], P(None, 'st'), may hold values from 0 to 33
- time_points: float32 [2048], replicated, may hold values from 0 to 1, as said below
- pattern: int32 [64, 9], P('st'), may hold values from 0 to 63, as said below
- site_blocks: int32 [4096, 4], P('st'), may hold values from 0 to 63, as said below
Outputs:
- solution: float32 [8192, 2048], P('st', 'tm')
- predicted: float32 [4096, 2048], P('st', 'tm')
Inputs may be any that keep to these rules, and one draw needn't show every extreme that they name: `pattern`: row b lists block b first, then blocks at most 4 away from b, one of them exactly 4 away. `site_blocks`: the home block of site j is j // 64; its list starts with the home block, then blocks at most 4 away from it, one of them exactly 4 away. `time_points`: column a holds a time between a / 2048 and (a + 1) / 2048.
All inputs are finite; a program needn't handle non-finite values.
Results may differ from a plain program's by a relative error of at most 0.0003.
Values sent between devices are 32-bit elements; how exact they have to be, the bound alone decides.
A program may use at most 128 MiB of HBM per device.

v0:
```python
import math

import jax
import jax.numpy as jnp
from jax import lax
from jax.sharding import PartitionSpec as P

BS = 128
REACH = 4
TREACH = 16
NNZ = 9
NNB = 4
NT = 2048
ITERS = 2


HIGHEST_PREC = lax.Precision.HIGHEST
NUGGET = 1.0


def with_halo(block, sides, width):
    for axis, dim in sides:
        count = lax.axis_size(axis)
        forward = [(i, i + 1) for i in range(count - 1)]
        backward = [(target, source) for source, target in forward]
        low = lax.ppermute(
            lax.slice_in_dim(block, block.shape[dim] - width, None, axis=dim), axis, forward
        )
        high = lax.ppermute(lax.slice_in_dim(block, 0, width, axis=dim), axis, backward)
        block = jnp.concatenate([low, block, high], axis=dim)
    return block


def wendland(radius):
    remain = jnp.maximum(1.0 - radius, 0.0)
    return remain * remain * remain * remain * (4.0 * radius + 1.0)


def time_weight(first, second):
    return 2.5 / math.sqrt(TREACH) * wendland(jnp.abs(first - second) * (NT / TREACH))


def shards(observed, station_xy, site_xy, time_points, pattern, site_blocks):
    row_count, tm_width = observed.shape
    blocks_here = pattern.shape[0]
    span = blocks_here + 2 * REACH
    st_pos = lax.axis_index("st")
    tm_pos = lax.axis_index("tm")
    own_times = lax.dynamic_slice_in_dim(time_points, tm_pos * tm_width, tm_width)
    padded_times = jnp.pad(time_points, (TREACH, TREACH), constant_values=-10.0)
    band_times = lax.dynamic_slice_in_dim(padded_times, tm_pos * tm_width, tm_width + 2 * TREACH)
    band_cols = time_weight(band_times[:, None], own_times[None, :])
    near_xy = with_halo(station_xy, (("st", 1),), REACH * BS)
    local_ids = pattern - st_pos * blocks_here + REACH
    near_groups = near_xy.reshape(2, span, BS)
    partner = near_groups[:, local_ids]
    own_xy = station_xy.reshape(2, blocks_here, BS)
    diff_x = own_xy[0][:, None, :, None] - partner[0][:, :, None, :]
    diff_y = own_xy[1][:, None, :, None] - partner[1][:, :, None, :]
    kernel_tiles = (
        2.5
        / math.sqrt(NNZ * BS)
        * wendland(jnp.sqrt(diff_x * diff_x + diff_y * diff_y + 0.0001) / (0.75 * REACH))
    )
    solution = jnp.zeros_like(observed)
    resid = observed
    history = []
    for sweep in range(ITERS):
        widened = with_halo(resid, (("tm", 1),), TREACH)
        padded = with_halo(
            jnp.dot(widened, band_cols, precision=HIGHEST_PREC, preferred_element_type=jnp.float32),
            (("st", 0),),
            REACH * BS,
        )
        grouped = padded.reshape(span, BS, tm_width)[local_ids]
        result = jnp.einsum("bkij,bkjt->bit", kernel_tiles, grouped, precision=HIGHEST_PREC)
        applied = result.reshape(row_count, tm_width) + NUGGET * resid
        inner_sum, energy = lax.psum(
            (jnp.sum(resid * applied), jnp.sum(applied * applied)), ("st", "tm")
        )
        step_size = inner_sum / (energy + 1e-06)
        solution = solution + step_size * resid
        resid = resid - step_size * applied
        history.append((step_size, padded))
    padded_smooth = history[0][0] * history[0][1]
    for step_size, padded in history[1:]:
        padded_smooth = padded_smooth + step_size * padded
    site_count = site_xy.shape[1]
    site_local = site_blocks - st_pos * blocks_here + REACH
    block_range = jnp.arange(span, dtype=jnp.int32)
    counts = jnp.sum(
        (site_local[:, :, None] == block_range[None, None, :]).astype(jnp.float32), axis=1
    )
    site_dx = site_xy[0][:, None] - near_xy[0][None, :]
    site_dy = site_xy[1][:, None] - near_xy[1][None, :]
    site_kernel = (
        2.5
        / math.sqrt(NNB * BS)
        * wendland(jnp.sqrt(site_dx * site_dx + site_dy * site_dy + 0.0001) / (0.75 * REACH))
    )
    weights = (site_kernel.reshape(site_count, span, BS) * counts[:, :, None]).reshape(
        site_count, span * BS
    )
    predicted = jnp.dot(
        weights, padded_smooth, precision=HIGHEST_PREC, preferred_element_type=jnp.float32
    )
    return (solution, predicted)


def solution(mesh):
    placed = (P("st", "tm"), P(None, "st"), P(None, "st"), P(), P("st", None), P("st", None))
    return jax.shard_map(
        shards,
        mesh=mesh,
        in_specs=placed,
        out_specs=(P("st", "tm"), P("st", "tm")),
        check_vma=False,
    )
```

profile of v0, /device:TPU:0, one launch (start us, length us, event | category | flops | bytes accessed | tf_op | source)
XLA Modules:
  0.0 286.8 jit_solution(16477419614664698337)
XLA Ops:
  0.6 1.4 fusion.103
  2.0 5.0 %collective-permute-start.2 = (f32[1024,16]{1,0:T(8,128)S(1)}, f32[1024,16]{1,0:T(8,128)S(1)}, u32[]{:S(2)}, u32[]{:S(2)}) collective-permute-start(f32[1024,16]{1,0:T(8,128)S(1)} %get-tuple-element.16), channel_id=1, source_target_pairs={{0,1},{1,2},{2,3},{4,5},{5,6},{6,7},{8,9},{9,10},{10,11},{12,13},{... | collective-permute-start | bytes 196616 | tf_op jit(solution)/shard_map/ppermute | solution.py:26
  7.0 1.3 collective-permute-start.3
  8.3 0.7 fusion.107
  9.0 1.4 collective-permute-start
  10.5 1.3 collective-permute-start.1
  11.8 0.7 compare_select_fusion
  12.5 0.1 reshape.68
  12.6 0.8 dynamic_slice.7
  13.3 0.8 pad_dynamic-slice_fusion
  14.1 4.0 %collective-permute-done.2 = f32[1024,16]{1,0:T(8,128)S(1)} collective-permute-done((f32[1024,16]{1,0:T(8,128)S(1)}, f32[1024,16]{1,0:T(8,128)S(1)}, u32[]{:S(2)}, u32[]{:S(2)}) %collective-permute-start.2) | collective-permute-done | bytes 65568 | tf_op jit(solution)/shard_map/ppermute | solution.py:26
  18.2 4.1 %collective-permute-done.3 = f32[1024,16]{1,0:T(8,128)S(1)} collective-permute-done((f32[1024,16]{1,0:T(8,128)S(1)}, f32[1024,16]{1,0:T(8,128)S(1)}, u32[]{:S(2)}, u32[]{:S(2)}) %collective-permute-start.3) | collective-permute-done | bytes 65568 | tf_op jit(solution)/shard_map/ppermute | solution.py:29
  22.3 7.2 %fusion.24 = f32[1024,512]{1,0:T(8,128)S(1)} fusion(f32[1024,16]{1,0:T(8,128)S(1)} %collective-permute-done.3, f32[1024,512]{1,0:T(8,128)} %param.6, f32[1024,16]{1,0:T(8,128)S(1)} %collective-permute-done.2, f32[512]{0:T(512)S(1)} %dynamic_slice.7, f32[544]{0:T(1024)S(1)} %pad_dynamic-slice_fusion), kind=kOutput, calls=%fused_computation.30 | convolution fusion | flops 3427008512 | bytes 4329600 | tf_op jit(solution)/shard_map/dot_general | solution.py:71
  29.5 1.3 fusion.102
  30.8 2.3 collective-permute-start.4
  33.1 1.5 collective-permute-start.5
  34.7 0.7 gather_fusion
  35.3 0.1 fusion.104
  35.4 3.1 %collective-permute-done.5 = f32[512,512]{1,0:T(8,128)} collective-permute-done((f32[512,512]{1,0:T(8,128)S(1)}, f32[512,512]{1,0:T(8,128)}, u32[]{:S(2)}, u32[]{:S(2)}) %collective-permute-start.5) | collective-permute-done | bytes 1048608 | tf_op jit(solution)/shard_map/ppermute | solution.py:29
  38.5 4.0 %pad_maximum_fusion = f32[2048,512]{1,0:T(8,128)} fusion(f32[512,512]{1,0:T(8,128)} %collective-permute-done.5, f32[1024,512]{1,0:T(8,128)S(1)} %fusion.24, f32[512,512]{1,0:T(8,128)} %collective-permute-done.4), kind=kLoop, calls=%fused_computation.13 | loop fusion | flops 2097152 | bytes 8388608 | tf_op jit(solution)/shard_map/concatenate | solution.py:30
  42.5 11.7 %gather_fusion.1 = f32[72,128,512]{2,1,0:T(8,128)} fusion(f32[16,128,512]{2,1,0:T(8,128)} %bitcast.49, s32[1024]{0:T(1024)S(1)} %pad_clamp_fusion), kind=kCustom, calls=%fused_computation.1 | custom fusion | bytes 37749024 | tf_op jit(solution)/shard_map/gather | solution.py:75
  54.3 18.1 %fusion.38 = f32[8,128,512,1]{2,1,3,0:T(8,128)S(1)} fusion(f32[8,9,128,512]{3,2,1,0:T(8,128)} %bitcast.51, f32[8,9,128]{2,1,0:T(8,128)S(1)} %get-tuple-element.28, f32[8,128]{1,0:T(8,128)S(1)} %bitcast.59, f32[8,9,128]{2,1,0:T(8,128)S(1)} %get-tuple-element.29, f32[8,128]{1,0:T(8,128)S(1)} %bitcast.57), kind=kOutput, calls=%fused_computation.43 | convolution fusion | flops 7266631680 | bytes 21053440 | tf_op jit(solution)/shard_map/bkij,bkjt->bit/dot_general | solution.py:76
  72.4 1.3 copy-done.3
  73.7 1.2 multiply_reduce_fusion.2
  74.9 59.9 %all-reduce.2 = (f32[]{:T(128)}, f32[]{:T(128)}) all-reduce(f32[]{:T(128)} %get-tuple-element.5, f32[]{:T(128)} %get-tuple-element.4), channel_id=1, replica_groups=mesh['st'=8,'tm'=4] {'st','tm'}, use_global_device_ids=true, to_apply=%region_1.2 | all-reduce | flops 2 | bytes 16 | tf_op jit(solution)/shard_map/psum | solution.py:78
  136.0 2.1 multiply_subtract_fusion
  138.1 0.2 fusion.101
  138.3 2.2 collective-permute-start.6
  140.5 0.0 copy-start.11
  140.5 1.5 collective-permute-start.7
  142.0 9.0 %collective-permute-done.6 = f32[1024,16]{1,0:T(8,128)S(1)} collective-permute-done((f32[1024,16]{1,0:T(8,128)S(1)}, f32[1024,16]{1,0:T(8,128)S(1)}, u32[]{:S(2)}, u32[]{:S(2)}) %collective-permute-start.6) | collective-permute-done | bytes 65568 | tf_op jit(solution)/shard_map/ppermute | solution.py:26
  151.0 4.2 %collective-permute-done.7 = f32[1024,16]{1,0:T(8,128)S(1)} collective-permute-done((f32[1024,16]{1,0:T(8,128)S(1)}, f32[1024,16]{1,0:T(8,128)S(1)}, u32[]{:S(2)}, u32[]{:S(2)}) %collective-permute-start.7) | collective-permute-done | bytes 65568 | tf_op jit(solution)/shard_map/ppermute | solution.py:29
  155.2 5.6 %fusion.30 = f32[1024,512]{1,0:T(8,128)S(1)} fusion(f32[1024,16]{1,0:T(8,128)S(1)} %collective-permute-done.7, f32[1024,512]{1,0:T(8,128)S(1)} %multiply_subtract_fusion, f32[1024,16]{1,0:T(8,128)S(1)} %collective-permute-done.6, f32[512]{0:T(512)S(1)} %dynamic_slice.7, f32[544]{0:T(1024)S(1)} %pad_dynamic-slice_fusion), kind=kOutput, calls=%fused_computation.36 | convolution fusion | flops 3427008512 | bytes 4329600 | tf_op jit(solution)/shard_map/dot_general | solution.py:71
  160.8 1.3 fusion.100
  162.1 0.5 copy-done.6
  162.6 2.2 collective-permute-start.8
  164.9 1.3 collective-permute-start.9
  166.2 0.1 copy.19
  166.4 0.1 collective-permute-done.8
  166.5 3.7 %collective-permute-done.9 = f32[512,512]{1,0:T(8,128)} collective-permute-done((f32[512,512]{1,0:T(8,128)S(1)}, f32[512,512]{1,0:T(8,128)}, u32[]{:S(2)}, u32[]{:S(2)}) %collective-permute-start.9) | collective-permute-done | bytes 1048608 | tf_op jit(solution)/shard_map/ppermute | solution.py:29
  170.3 4.7 %pad_maximum_fusion.1 = f32[2048,512]{1,0:T(8,128)} fusion(f32[512,512]{1,0:T(8,128)} %collective-permute-done.9, f32[1024,512]{1,0:T(8,128)} %copy-done.6, f32[512,512]{1,0:T(8,128)} %collective-permute-done.8), kind=kLoop, calls=%fused_computation.14 | loop fusion | flops 2097152 | bytes 8388608 | tf_op jit(solution)/shard_map/concatenate | solution.py:30
  174.9 11.7 %gather_fusion.2 = f32[72,128,512]{2,1,0:T(8,128)} fusion(f32[16,128,512]{2,1,0:T(8,128)} %bitcast.48, s32[1024]{0:T(1024)S(1)} %pad_clamp_fusion), kind=kCustom, calls=%fused_computation.2 | custom fusion | bytes 37749024 | tf_op jit(solution)/shard_map/gather | solution.py:75
  186.7 18.1 %fusion.36 = f32[8,128,512,1]{2,1,3,0:T(8,128)S(1)} fusion(f32[8,9,128,512]{3,2,1,0:T(8,128)} %bitcast.50, f32[8,9,128]{2,1,0:T(8,128)S(1)} %get-tuple-element.28, f32[8,128]{1,0:T(8,128)S(1)} %bitcast.60, f32[8,9,128]{2,1,0:T(8,128)S(1)} %copy-done.10, f32[8,128]{1,0:T(8,128)S(1)} %bitcast.58), kind=kOutput, calls=%fused_computation.42 | convolution fusion | flops 7266631680 | bytes 21053440 | tf_op jit(solution)/shard_map/bkij,bkjt->bit/dot_general | solution.py:76
  204.8 1.2 multiply_reduce_fusion
  206.0 60.0 %all-reduce.1 = (f32[]{:T(128)}, f32[]{:T(128)}) all-reduce(f32[]{:T(128)} %get-tuple-element.3, f32[]{:T(128)} %get-tuple-element.2), channel_id=1, replica_groups=mesh['st'=8,'tm'=4] {'st','tm'}, use_global_device_ids=true, to_apply=%region_5.6 | all-reduce | flops 2 | bytes 16 | tf_op jit(solution)/shard_map/psum | solution.py:78
  267.2 3.6 %multiply_add_fusion = f32[1024,512]{1,0:T(8,128)} fusion(f32[1024,512]{1,0:T(8,128)} %copy-done.1, f32[1024,512]{1,0:T(8,128)S(1)} %copy-done, f32[]{:T(128)S(6)} %div.21, f32[]{:T(128)S(6)} %div.20), kind=kLoop, calls=%fused_computation.58 | loop fusion | flops 1572864 | bytes 6291464 | tf_op jit(solution)/shard_map/add | solution.py:82
  270.8 1.1 mul.206
  271.9 14.4 %fusion.5 = f32[512,512]{1,0:T(8,128)} fusion(f32[64,8,16,128]{3,2,1,0:T(8,128)S(1)} %bitcast.52, f32[]{:T(128)S(6)} %div.21, f32[]{:T(128)S(6)} %div.20, f32[2048]{0:T(1024)S(1)} %bitcast.56, f32[512]{0:T(512)S(1)} %bitcast.62, f32[2048]{0:T(1024)S(1)} %bitcast.55, f32[512]{0:T(512)S(1)} %bitcast.61, f32[512,512]{1,0:T(8,128)} %collective-permute-done.9, ...), kind=kOutput, calls=%fused_computation.10 | convolution fusion | flops 6467616768 | bytes 13651976 | tf_op jit(solution)/shard_map/dot_general | solution.py:104
  (36 shorter events, 0.2 us)
Async XLA Ops:
  2.0 16.1 %collective-permute-start.2 = (f32[1024,16]{1,0:T(8,128)S(1)}, f32[1024,16]{1,0:T(8,128)S(1)}, u32[]{:S(2)}, u32[]{:S(2)}) collective-permute-start(f32[1024,16]{1,0:T(8,128)S(1)} %get-tuple-element.16), channel_id=1, source_target_pairs={{0,1},{1,2},{2,3},{4,5},{5,6},{6,7},{8,9},{9,10},{10,11},{12,13},{... | collective-permute-start | bytes 196616 | tf_op jit(solution)/shard_map/ppermute | solution.py:26
  7.0 15.3 %collective-permute-start.3 = (f32[1024,16]{1,0:T(8,128)S(1)}, f32[1024,16]{1,0:T(8,128)S(1)}, u32[]{:S(2)}, u32[]{:S(2)}) collective-permute-start(f32[1024,16]{1,0:T(8,128)S(1)} %get-tuple-element.17), channel_id=1, source_target_pairs={{1,0},{2,1},{3,2},{5,4},{6,5},{7,6},{9,8},{10,9},{11,10},{13,12},{... | collective-permute-start | bytes 196616 | tf_op jit(solution)/shard_map/ppermute | solution.py:29
  9.0 25.6 %collective-permute-start = (f32[2,512]{1,0:T(2,128)S(1)}, f32[2,512]{1,0:T(2,128)S(1)}, u32[]{:S(2)}, u32[]{:S(2)}) collective-permute-start(f32[2,512]{1,0:T(2,128)S(1)} %get-tuple-element.25), channel_id=1, source_target_pairs={{0,4},{4,8},{8,12},{12,16},{16,20},{20,24},{24,28},{1,5},{5,9},{9,... | collective-permute-start | bytes 12296 | tf_op jit(solution)/shard_map/ppermute | solution.py:26
  10.5 24.1 %collective-permute-start.1 = (f32[2,512]{1,0:T(2,128)S(1)}, f32[2,512]{1,0:T(2,128)S(1)}, u32[]{:S(2)}, u32[]{:S(2)}) collective-permute-start(f32[2,512]{1,0:T(2,128)S(1)} %get-tuple-element.24), channel_id=1, source_target_pairs={{4,0},{8,4},{12,8},{16,12},{20,16},{24,20},{28,24},{5,1},{9,5},{13... | collective-permute-start | bytes 12296 | tf_op jit(solution)/shard_map/ppermute | solution.py:29
  14.1 20.5 %copy-start.8 = (f32[2,1024]{1,0:T(2,128)S(1)}, f32[2,1024]{1,0:T(2,128)}, u32[]{:S(2)}) copy-start(f32[2,1024]{1,0:T(2,128)} %param.7) | copy-start | bytes 24580
  29.5 13.0 %copy-start.4 = (f32[1024,512]{1,0:T(8,128)}, f32[1024,512]{1,0:T(8,128)S(1)}, u32[]{:S(2)}) copy-start(f32[1024,512]{1,0:T(8,128)S(1)} %fusion.24) | copy-start | bytes 6291460
  30.8 4.6 %collective-permute-start.4 = (f32[512,512]{1,0:T(8,128)}, f32[512,512]{1,0:T(8,128)}, u32[]{:S(2)}, u32[]{:S(2)}) collective-permute-start(f32[512,512]{1,0:T(8,128)} %get-tuple-element.14), channel_id=1, source_target_pairs={{0,4},{4,8},{8,12},{12,16},{16,20},{20,24},{24,28},{1,5},{5,9},{9,... | collective-permute-start | bytes 3145736 | tf_op jit(solution)/shard_map/ppermute | solution.py:26
  33.1 5.4 %collective-permute-start.5 = (f32[512,512]{1,0:T(8,128)S(1)}, f32[512,512]{1,0:T(8,128)}, u32[]{:S(2)}, u32[]{:S(2)}) collective-permute-start(f32[512,512]{1,0:T(8,128)S(1)} %get-tuple-element.15), channel_id=1, source_target_pairs={{4,0},{8,4},{12,8},{16,12},{20,16},{24,20},{28,24},{5,1},{9,5},{13... | collective-permute-start | bytes 3145736 | tf_op jit(solution)/shard_map/ppermute | solution.py:29
  35.4 18.8 %copy-start.9 = (f32[8,9,128]{2,1,0:T(8,128)}, f32[8,9,128]{2,1,0:T(8,128)S(1)}, u32[]{:S(2)}) copy-start(f32[8,9,128]{2,1,0:T(8,128)S(1)} %get-tuple-element.29) | copy-start | bytes 110596
  54.3 19.5 %copy-start = (f32[1024,512]{1,0:T(8,128)S(1)}, f32[1024,512]{1,0:T(8,128)}, u32[]{:S(2)}) copy-start(f32[1024,512]{1,0:T(8,128)} %param.6) | copy-start | bytes 6291460
  72.4 1.3 copy-start.3
  138.1 22.7 %copy-start.1 = (f32[1024,512]{1,0:T(8,128)}, f32[1024,512]{1,0:T(8,128)S(1)}, u32[]{:S(2)}) copy-start(f32[1024,512]{1,0:T(8,128)S(1)} %multiply_subtract_fusion) | copy-start | bytes 6291460
  138.3 12.7 %collective-permute-start.6 = (f32[1024,16]{1,0:T(8,128)S(1)}, f32[1024,16]{1,0:T(8,128)S(1)}, u32[]{:S(2)}, u32[]{:S(2)}) collective-permute-start(f32[1024,16]{1,0:T(8,128)S(1)} %get-tuple-element.12), channel_id=1, source_target_pairs={{0,1},{1,2},{2,3},{4,5},{5,6},{6,7},{8,9},{9,10},{10,11},{12,13},{... | collective-permute-start | bytes 196616 | tf_op jit(solution)/shard_map/ppermute | solution.py:26
  140.5 25.7 %copy-start.11 = (s32[512,4]{0,1:T(4,128)S(1)}, s32[512,4]{0,1:T(4,128)}, u32[]{:S(2)}) copy-start(s32[512,4]{0,1:T(4,128)} %param.11) | copy-start | bytes 24580
  140.5 14.6 %collective-permute-start.7 = (f32[1024,16]{1,0:T(8,128)S(1)}, f32[1024,16]{1,0:T(8,128)S(1)}, u32[]{:S(2)}, u32[]{:S(2)}) collective-permute-start(f32[1024,16]{1,0:T(8,128)S(1)} %get-tuple-element.13), channel_id=1, source_target_pairs={{1,0},{2,1},{3,2},{5,4},{6,5},{7,6},{9,8},{10,9},{11,10},{13,12},{... | collective-permute-start | bytes 196616 | tf_op jit(solution)/shard_map/ppermute | solution.py:29
  160.8 1.8 copy-start.6
  160.8 5.5 %copy-start.12 = (f32[2,512]{1,0:T(2,128)S(1)}, f32[2,512]{1,0:T(2,128)}, u32[]{:S(2)}) copy-start(f32[2,512]{1,0:T(2,128)} %param.8) | copy-start | bytes 12292
  162.6 3.9 %collective-permute-start.8 = (f32[512,512]{1,0:T(8,128)}, f32[512,512]{1,0:T(8,128)}, u32[]{:S(2)}, u32[]{:S(2)}) collective-permute-start(f32[512,512]{1,0:T(8,128)} %get-tuple-element.10), channel_id=1, source_target_pairs={{0,4},{4,8},{8,12},{12,16},{16,20},{20,24},{24,28},{1,5},{5,9},{9,... | collective-permute-start | bytes 3145736 | tf_op jit(solution)/shard_map/ppermute | solution.py:26
  164.9 5.4 %collective-permute-start.9 = (f32[512,512]{1,0:T(8,128)S(1)}, f32[512,512]{1,0:T(8,128)}, u32[]{:S(2)}, u32[]{:S(2)}) collective-permute-start(f32[512,512]{1,0:T(8,128)S(1)} %get-tuple-element.11), channel_id=1, source_target_pairs={{4,0},{8,4},{12,8},{16,12},{20,16},{24,20},{28,24},{5,1},{9,5},{13... | collective-permute-start | bytes 3145736 | tf_op jit(solution)/shard_map/ppermute | solution.py:29
  174.9 11.8 %copy-start.10 = (f32[8,9,128]{2,1,0:T(8,128)S(1)}, f32[8,9,128]{2,1,0:T(8,128)}, u32[]{:S(2)}) copy-start(f32[8,9,128]{2,1,0:T(8,128)} %copy-done.9) | copy-start | bytes 110596
  186.7 18.1 %copy-start.2 = (f32[1024,512]{1,0:T(8,128)S(1)}, f32[1024,512]{1,0:T(8,128)}, u32[]{:S(2)}) copy-start(f32[1024,512]{1,0:T(8,128)} %copy-done.1) | copy-start | bytes 6291460
  267.1 4.8 %copy-start.5 = (f32[1024,512]{1,0:T(8,128)S(1)}, f32[1024,512]{1,0:T(8,128)}, u32[]{:S(2)}) copy-start(f32[1024,512]{1,0:T(8,128)} %copy-done.4) | copy-start | bytes 6291460
  267.2 4.8 %copy-start.7 = (f32[1024,512]{1,0:T(8,128)S(1)}, f32[1024,512]{1,0:T(8,128)}, u32[]{:S(2)}) copy-start(f32[1024,512]{1,0:T(8,128)} %copy-done.6) | copy-start | bytes 6291460
where the time goes:
time: 292 us; the launch traced here: 287 us
  blocking collectives  120 us (41%)
  matrix products  63.5 us (22%)
  local copies, waits for them, and re-layouts  33.9 us (12%)
  waiting for transfers between devices  28.3 us (10%)
  starting transfers between devices  20 us (7%)
  other arithmetic  17.4 us (6%)
  between operations  3.87 us (1%)
    psum x2, blocking collectives, shards(): lax.psum((jnp.sum(resid * applied), jnp.sum(applied * applied)), ('st', '...  120 us
    dot_general x2, matrix products, shards(): jnp.einsum('bkij,bkjt->bit', kernel_tiles, grouped, precision=HIGHEST_PREC)  36.2 us
    gather x2, local copies, waits for them, and re-layouts, shards(): grouped = padded.reshape(span, BS, tm_width)[local_ids]  23.5 us
    ppermute x5, waiting for transfers between devices, with_halo(): lax.ppermute(lax.slice_in_dim(block, 0, width, axis=dim), axis, backward)  15.1 us
    dot_general x1, matrix products, shards(): jnp.dot(weights, padded_smooth, precision=HIGHEST_PREC, preferred_element...  14.4 us
    ppermute x5, starting transfers between devices, with_halo(): lax.ppermute(lax.slice_in_dim(block, block.shape[dim] - width, None, axis...  13.2 us
    ppermute x5, waiting for transfers between devices, with_halo(): lax.ppermute(lax.slice_in_dim(block, block.shape[dim] - width, None, axis...  13.2 us
    dot_general x2, matrix products, shards(): jnp.dot(widened, band_cols, precision=HIGHEST_PREC, preferred_element_typ...  12.8 us
  transfers between devices with their start and end apart: 10, of which 7 were waited for; matrix products, arithmetic and copies ran while one was open for 4% of the time, Pallas kernels for 0%

commit v1 on v0

v1 whole, which is shorter than its diff:
```python
import functools
import math

import jax
import jax.numpy as jnp
from jax import lax
from jax.experimental import pallas as pl
from jax.experimental.pallas import tpu as pltpu
from jax.sharding import PartitionSpec as P

BS = 128
REACH = 4
TREACH = 16
NNZ = 9
NNB = 4
NT = 2048
ITERS = 2
NUGGET = 1.0
MESH = pl.DeviceIdType.MESH
F32 = jnp.float32
BF16 = jnp.bfloat16


def wendland(radius):
    remain = jnp.maximum(1.0 - radius, 0.0)
    square = remain * remain
    return square * square * (4.0 * radius + 1.0)


def split(x):
    hi = x.astype(BF16)
    return hi, (x - hi.astype(F32)).astype(BF16)


def dot(a, b):
    return jnp.dot(a, b, preferred_element_type=F32)


def dot3(ah, al, bh, bl):
    return dot(ah, bh) + dot(ah, bl) + dot(al, bh)


def column(row):
    return jnp.transpose(jnp.broadcast_to(row, (BS, BS)))


def fold(x):
    rows, cols = x.shape
    x = jnp.sum(x.reshape(rows // 8, 8, cols), axis=0)
    total = x[:, :BS]
    for start in range(BS, cols, BS):
        total = total + x[:, start : start + BS]
    return total


def kernel(
    st_n,
    tm_n,
    obs,
    sxy,
    pxy,
    times,
    pattern,
    site_blocks,
    sol,
    pred,
    near,
    nx,
    ny,
    edge_out,
    edge_in,
    band_hi,
    band_lo,
    edge_band,
    pad,
    pad_hi,
    pad_lo,
    k_hi,
    k_lo,
    w_hi,
    w_lo,
    field,
    resid,
    pred_next,
    sums_tm,
    sums_st,
    xy_send,
    xy_recv,
    edge_send,
    edge_recv,
    pad_send,
    pad_recv,
    tm_send,
    tm_recv,
    st_send,
    st_recv,
):
    rows, width = obs.shape
    blocks = pattern.shape[0]
    groups = sxy.shape[0]
    sites = site_blocks.shape[0]
    margin = REACH * BS
    span = blocks + 2 * REACH
    chunk = 2 * BS
    pairs = blocks // 2
    lanes = width // BS
    st = lax.axis_index("st")
    tm = lax.axis_index("tm")
    has_low, has_high = st > 0, st < st_n - 1
    has_left, has_right = tm > 0, tm < tm_n - 1

    barrier = pltpu.get_barrier_semaphore()
    for d in range(1, st_n):
        pl.semaphore_signal(barrier, inc=1, device_id={"st": (st + d) % st_n}, device_id_type=MESH)
    for d in range(1, tm_n):
        pl.semaphore_signal(barrier, inc=1, device_id={"tm": (tm + d) % tm_n}, device_id_type=MESH)

    def shift(src, dst, send, recv, axis, pos, count, step):
        return pltpu.make_async_remote_copy(
            src_ref=src,
            dst_ref=dst,
            send_sem=send,
            recv_sem=recv,
            device_id={axis: (pos + step + count) % count},
            device_id_type=MESH,
        )

    def xy_copy(up):
        if up:
            return shift(sxy.at[groups - 1], near.at[0], xy_send.at[0], xy_recv.at[0], "st", st, st_n, 1)
        return shift(sxy.at[0], near.at[1], xy_send.at[1], xy_recv.at[1], "st", st, st_n, -1)

    def edge_copy(it, up):
        k = 1 if up else 0
        step = 1 if up else -1
        return shift(
            edge_out.at[it, k], edge_in.at[it, k], edge_send.at[it, k], edge_recv.at[it, k],
            "tm", tm, tm_n, step,
        )

    halves = margin // chunk

    def pad_copy(it, up, part):
        k = 1 if up else 0
        if up:
            source = margin + rows - margin + part * chunk
            target = part * chunk
        else:
            source = margin + part * chunk
            target = margin + rows + part * chunk
        return shift(
            pad.at[it, pl.ds(source, chunk)],
            pad.at[it, pl.ds(target, chunk)],
            pad_send.at[it, k, part],
            pad_recv.at[it, k, part],
            "st", st, st_n, 1 if up else -1,
        )

    def take_edges(source, it):
        for b in range(blocks):
            here = slice(b * BS, (b + 1) * BS)
            edge_out[it, 0, :, here] = jnp.transpose(source[here, :BS])[:TREACH]
            edge_out[it, 1, :, here] = jnp.transpose(source[here, width - BS :])[BS - TREACH :]

    def start_edges(it):
        @pl.when(has_left)
        def _():
            edge_copy(it, False).start()

        @pl.when(has_right)
        def _():
            edge_copy(it, True).start()

    def finish_edges(it):
        @pl.when(has_left)
        def _():
            edge_copy(it, True).wait_recv()

        @pl.when(has_right)
        def _():
            edge_copy(it, False).wait_recv()

        @pl.when(tm == 0)
        def _():
            edge_in[it, 1] = jnp.zeros_like(edge_in[it, 1])

        @pl.when(tm == tm_n - 1)
        def _():
            edge_in[it, 0] = jnp.zeros_like(edge_in[it, 0])

    def mix(source, it, left, right):
        def stack(x):
            hi, lo = split(x)
            return jnp.concatenate([hi, hi, lo], axis=0)

        for k, value in ((1, left), (0, right)):
            edges = stack(value)
            lane = 0 if k == 1 else width - BS
            for c in range(rows // chunk):
                here = pl.ds(margin + c * chunk, chunk)
                add = lax.dot_general(
                    edges[:, c * chunk : (c + 1) * chunk],
                    edge_band[k],
                    (((0,), (0,)), ((), ())),
                    preferred_element_type=F32,
                )
                pad[it, here, lane : lane + BS] = add
        order = []
        for part in range(halves):
            order.append((part, False, part))
            order.append((rows // chunk - halves + part, True, part))
        for c, up, part in order:
            hi, lo = split(source[c * chunk : (c + 1) * chunk, :])
            here = pl.ds(margin + c * chunk, chunk)
            mixed = dot3(hi, lo, band_hi[...], band_lo[...])
            first = mixed[:, :BS] + pad[it, here, :BS]
            last = mixed[:, width - BS :] + pad[it, here, width - BS :]
            mixed = jnp.concatenate([first, mixed[:, BS : width - BS], last], axis=1)
            pad[it, here, :] = mixed

            @pl.when(has_high if up else has_low)
            def _(up=up, part=part):
                pad_copy(it, up, part).start()

            pad_hi[it, here, :], pad_lo[it, here, :] = split(mixed)

    def receive(it, up, part):
        begin = part * chunk if up else margin + rows + part * chunk
        here = pl.ds(begin, chunk)

        @pl.when(has_low if up else has_high)
        def _():
            pad_copy(it, up, part).wait_recv()
            pad_hi[it, here, :], pad_lo[it, here, :] = split(pad[it, here, :])

        @pl.when(st == (0 if up else st_n - 1))
        def _():
            zero = jnp.zeros((chunk, width), BF16)
            pad_hi[it, here, :] = zero
            pad_lo[it, here, :] = zero

    half = min(width, 256)

    def apply_part(it, p, begin, end, col):
        here = slice(p * chunk, (p + 1) * chunk)
        cols = slice((begin - 2 * p) * BS, (end - 2 * p) * BS)
        ins = slice(begin * BS, end * BS)
        return dot3(
            k_hi[here, cols], k_lo[here, cols], pad_hi[it, ins, col], pad_lo[it, ins, col]
        )

    def apply_own(it):
        @pl.loop(0, width // half)
        def _(n):
            col = pl.ds(pl.multiple_of(n * half, half), half)
            for p in range(pairs):
                begin = max(2 * p, REACH)
                end = min(2 * p + 2 + 2 * REACH, REACH + blocks)
                field[p * chunk : (p + 1) * chunk, col] = apply_part(it, p, begin, end, col)

    def apply_halo(it, p, source):
        begin = max(2 * p, REACH)
        end = min(2 * p + 2 + 2 * REACH, REACH + blocks)
        here = slice(p * chunk, (p + 1) * chunk)
        inner = jnp.zeros((8, BS), F32)
        energy = jnp.zeros((8, BS), F32)
        for n in range(width // half):
            col = slice(n * half, (n + 1) * half)
            value = field[here, col]
            if 2 * p < begin:
                value = value + apply_part(it, p, 2 * p, begin, col)
            if end < 2 * p + 2 + 2 * REACH:
                value = value + apply_part(it, p, end, 2 * p + 2 + 2 * REACH, col)
            old = source[here, col]
            value = value + NUGGET * old
            field[here, col] = value
            inner = inner + fold(old * value)
            energy = energy + fold(value * value)
        return inner, energy

    def finish_apply(it, source):
        for part in range(halves):
            receive(it, True, part)
            receive(it, False, part)
        inner = jnp.zeros((8, BS), F32)
        energy = jnp.zeros((8, BS), F32)
        for p in range(pairs):
            one, two = apply_halo(it, p, source)
            inner, energy = inner + one, energy + two
        sums_tm[it, 0, :8] = inner
        sums_tm[it, 0, 8:] = energy

    def sum_copy(it, axis, d):
        if axis == "tm":
            return shift(sums_tm.at[it, 0], sums_tm.at[it, d], tm_send.at[it, d - 1],
                         tm_recv.at[it, d - 1], "tm", tm, tm_n, d)
        return shift(sums_st.at[it, 0], sums_st.at[it, d], st_send.at[it, d - 1],
                     st_recv.at[it, d - 1], "st", st, st_n, d)

    def start_sum(it, axis):
        for d in range(1, tm_n if axis == "tm" else st_n):
            sum_copy(it, axis, d).start()

    def finish_sum(it, axis):
        count, pos, buf = (tm_n, tm, sums_tm) if axis == "tm" else (st_n, st, sums_st)
        for d in range(1, count):
            sum_copy(it, axis, d).wait_recv()
        total = buf[it, pos % count]
        for j in range(1, count):
            total = total + buf[it, (pos - j + count) % count]
        return total

    def step_of(it):
        total = finish_sum(it, "st")
        inner = jnp.sum(jnp.sum(total[:8], axis=0, keepdims=True), axis=1, keepdims=True)
        energy = jnp.sum(jnp.sum(total[8:], axis=0, keepdims=True), axis=1, keepdims=True)
        return inner / (energy + 1e-06)

    take_edges(obs, 0)
    pl.semaphore_wait(barrier, st_n - 1 + tm_n - 1)
    start_edges(0)

    @pl.when(has_high)
    def _():
        xy_copy(True).start()

    @pl.when(has_low)
    def _():
        xy_copy(False).start()

    def time_row(i):
        count = times.shape[0]
        return times[pl.ds((tm * lanes + i + count) % count, 1), :]

    def time_tile(i, j):
        apart = jnp.abs(column(time_row(i)) - time_row(j))
        return 2.5 / math.sqrt(TREACH) * wendland(apart * (NT / TREACH))

    for i in range(lanes):
        for j in range(lanes):
            a = slice(i * BS, (i + 1) * BS)
            b = slice(j * BS, (j + 1) * BS)
            if abs(i - j) <= 1:
                band_hi[a, b], band_lo[a, b] = split(time_tile(i, j))
            else:
                band_hi[a, b] = jnp.zeros((BS, BS), BF16)
                band_lo[a, b] = jnp.zeros((BS, BS), BF16)
    for k, tile in (
        (1, time_tile(-1, 0)[BS - TREACH :]),
        (0, time_tile(lanes, lanes - 1)[:TREACH]),
    ):
        hi, lo = split(tile)
        edge_band[k] = jnp.concatenate([hi, lo, hi], axis=0)

    finish_edges(0)
    mix(obs, 0, edge_in[0, 1], edge_in[0, 0])

    @pl.when(has_low)
    def _():
        xy_copy(True).wait_recv()

    @pl.when(has_high)
    def _():
        xy_copy(False).wait_recv()

    @pl.when(st == 0)
    def _():
        near[0] = jnp.zeros_like(near[0])

    @pl.when(st == st_n - 1)
    def _():
        near[1] = jnp.zeros_like(near[1])

    for c, out in enumerate((nx, ny)):
        out[:REACH] = near[0, c]
        for g in range(groups):
            out[REACH * (g + 1) : REACH * (g + 2)] = sxy[g, c]
        out[REACH * (groups + 1) :] = near[1, c]

    lane_ids = lax.broadcasted_iota(jnp.int32, (BS, BS), 1)
    ids = pattern[...]
    k_counts = jnp.zeros((blocks, BS), F32)
    for s in range(NNZ):
        hit = ids[:, s : s + 1] == lane_ids[:blocks] + (st * blocks - REACH)
        k_counts = k_counts + hit.astype(F32)

    def weight(xcol, ycol, block, scale):
        dx = xcol - nx[pl.ds(block, 1), :]
        dy = ycol - ny[pl.ds(block, 1), :]
        radius = jnp.sqrt(dx * dx + dy * dy + 0.0001) * (1.0 / (0.75 * REACH))
        return scale * wendland(radius)

    for p in range(pairs):
        for q in range(2):
            b = 2 * p + q
            here = slice(b * BS, (b + 1) * BS)
            xcol = column(nx[REACH + b : REACH + b + 1, :])
            ycol = column(ny[REACH + b : REACH + b + 1, :])
            gap = (2 * REACH + 1 if q == 0 else 0) * BS
            k_hi[here, gap : gap + BS] = jnp.zeros((BS, BS), BF16)
            k_lo[here, gap : gap + BS] = jnp.zeros((BS, BS), BF16)
            for k in range(2 * REACH + 1):
                tile = weight(xcol, ycol, b + k, 2.5 / math.sqrt(NNZ * BS))
                tile = tile * k_counts[b : b + 1, b + k : b + k + 1]
                cols = slice((q + k) * BS, (q + k + 1) * BS)
                k_hi[here, cols], k_lo[here, cols] = split(tile)

    apply_own(0)
    finish_apply(0, obs)
    start_sum(0, "tm")
    take_edges(field, 1)
    start_edges(1)
    sums_st[0, 0] = finish_sum(0, "tm")
    start_sum(0, "st")

    site_rows = sites // pxy.shape[1]
    per_group = BS // (sites // blocks)
    wide = w_hi.shape[1] // BS
    site_chunks = pxy.shape[1]
    chunks_per = chunk // BS

    def site_tiles(h):
        here = slice(h * BS, (h + 1) * BS)
        base = (h // chunks_per) * chunks_per * per_group
        xcol = column(pxy[0, h : h + 1, :])
        ycol = column(pxy[1, h : h + 1, :])
        listed = site_blocks[here, :]
        counts = jnp.zeros((BS, BS), F32)
        for s in range(NNB):
            hit = listed[:, s : s + 1] == lane_ids + (st * blocks - REACH + base)
            counts = counts + hit.astype(F32)
        first = h * per_group - base
        for k in range(wide):
            cols = slice(k * BS, (k + 1) * BS)
            if first <= k < first + per_group + 2 * REACH:
                tile = weight(xcol, ycol, base + k, 2.5 / math.sqrt(NNB * BS))
                tile = tile * counts[:, k : k + 1]
                w_hi[here, cols], w_lo[here, cols] = split(tile)
            else:
                w_hi[here, cols] = jnp.zeros((BS, BS), BF16)
                w_lo[here, cols] = jnp.zeros((BS, BS), BF16)

    for h in range(site_chunks):
        site_tiles(h)

    finish_edges(1)
    step0 = step_of(0)
    for c in range(rows // chunk):
        here = slice(c * chunk, (c + 1) * chunk)
        resid[here, :] = obs[here, :] - step0 * field[here, :]
    mix(
        resid,
        1,
        edge_in[0, 1] - step0 * edge_in[1, 1],
        edge_in[0, 0] - step0 * edge_in[1, 0],
    )

    def predict(it, out):
        @pl.loop(0, width // half)
        def _(n):
            col = pl.ds(pl.multiple_of(n * half, half), half)
            for g in range(sites // chunk):
                here = slice(g * chunk, (g + 1) * chunk)
                base = g * chunks_per * per_group * BS
                ins = slice(base, base + wide * BS)
                out[here, col] = dot3(
                    w_hi[here, :], w_lo[here, :], pad_hi[it, ins, col], pad_lo[it, ins, col]
                )

    apply_own(1)
    predict(0, pred)
    finish_apply(1, resid)
    start_sum(1, "tm")
    sums_st[1, 0] = finish_sum(1, "tm")
    start_sum(1, "st")
    predict(1, pred_next)
    step1 = step_of(1)
    for c in range(rows // chunk):
        here = slice(c * chunk, (c + 1) * chunk)
        sol[here, :] = step0 * obs[here, :] + step1 * resid[here, :]
    for c in range(sites // chunk):
        here = slice(c * chunk, (c + 1) * chunk)
        pred[here, :] = step0 * pred[here, :] + step1 * pred_next[here, :]

    @pl.when(has_high)
    def _():
        xy_copy(True).wait_send()
        for it in range(ITERS):
            for part in range(halves):
                pad_copy(it, True, part).wait_send()

    @pl.when(has_low)
    def _():
        xy_copy(False).wait_send()
        for it in range(ITERS):
            for part in range(halves):
                pad_copy(it, False, part).wait_send()

    @pl.when(has_left)
    def _():
        for it in range(ITERS):
            edge_copy(it, False).wait_send()

    @pl.when(has_right)
    def _():
        for it in range(ITERS):
            edge_copy(it, True).wait_send()

    for it in range(ITERS):
        for axis, count in (("tm", tm_n), ("st", st_n)):
            for d in range(1, count):
                sum_copy(it, axis, d).wait_send()


def shards(st_n, tm_n, observed, station_xy, site_xy, time_points, pattern, site_blocks):
    rows, width = observed.shape
    blocks = pattern.shape[0]
    sites = site_blocks.shape[0]
    padded = rows + 2 * REACH * BS
    groups = blocks // REACH
    per_group = BS // (sites // blocks)
    wide = (2 * per_group + 2 * REACH) * BS
    halves = REACH // 2
    sxy = station_xy.reshape(2, groups, REACH, BS).transpose(1, 0, 2, 3)
    pxy = site_xy.reshape(2, sites // BS, BS)
    times = time_points.reshape(-1, BS)
    vmem = pl.BlockSpec(memory_space=pltpu.VMEM)
    dma = pltpu.SemaphoreType.DMA
    return pl.pallas_call(
        functools.partial(kernel, st_n, tm_n),
        out_shape=(
            jax.ShapeDtypeStruct((rows, width), F32),
            jax.ShapeDtypeStruct((sites, width), F32),
        ),
        in_specs=[vmem] * 6,
        out_specs=(vmem, vmem),
        scratch_shapes=[
            pltpu.VMEM((2, 2, REACH, BS), F32),
            pltpu.VMEM((blocks + 2 * REACH, BS), F32),
            pltpu.VMEM((blocks + 2 * REACH, BS), F32),
            pltpu.VMEM((ITERS, 2, TREACH, rows), F32),
            pltpu.VMEM((ITERS, 2, TREACH, rows), F32),
            pltpu.VMEM((width, width), BF16),
            pltpu.VMEM((width, width), BF16),
            pltpu.VMEM((2, 3 * TREACH, BS), BF16),
            pltpu.VMEM((ITERS, padded, width), F32),
            pltpu.VMEM((ITERS, padded, width), BF16),
            pltpu.VMEM((ITERS, padded, width), BF16),
            pltpu.VMEM((rows, (2 + 2 * REACH) * BS), BF16),
            pltpu.VMEM((rows, (2 + 2 * REACH) * BS), BF16),
            pltpu.VMEM((sites, wide), BF16),
            pltpu.VMEM((sites, wide), BF16),
            pltpu.VMEM((rows, width), F32),
            pltpu.VMEM((rows, width), F32),
            pltpu.VMEM((sites, width), F32),
            pltpu.VMEM((ITERS, tm_n, 16, BS), F32),
            pltpu.VMEM((ITERS, st_n, 16, BS), F32),
            dma((2,)),
            dma((2,)),
            dma((ITERS, 2)),
            dma((ITERS, 2)),
            dma((ITERS, 2, halves)),
            dma((ITERS, 2, halves)),
            dma((ITERS, tm_n - 1)),
            dma((ITERS, tm_n - 1)),
            dma((ITERS, st_n - 1)),
            dma((ITERS, st_n - 1)),
        ],
        compiler_params=pltpu.CompilerParams(
            collective_id=0, has_side_effects=True, vmem_limit_bytes=60 * 1024 * 1024
        ),
    )(observed, sxy, pxy, times, pattern, site_blocks)


def solution(mesh):
    placed = (P("st", "tm"), P(None, "st"), P(None, "st"), P(), P("st", None), P("st", None))
    return jax.shard_map(
        functools.partial(shards, mesh.shape["st"], mesh.shape["tm"]),
        mesh=mesh,
        in_specs=placed,
        out_specs=(P("st", "tm"), P("st", "tm")),
        check_vma=False,
    )
```

time: 292 us -> 90.2 us (0.31); the launches traced: 287 us -> 89.9 us
  blocking collectives: 120 us -> 0 us
  Pallas kernels: 0 us -> 80.9 us
  matrix products: 63.5 us -> 0 us
  waiting for transfers between devices: 28.3 us -> 0 us
  local copies, waits for them, and re-layouts: 33.9 us -> 8.3 us
  starting transfers between devices: 20 us -> 0 us
  other arithmetic: 17.4 us -> 0 us
  between operations: 3.87 us -> 0.65 us
    psum x2 -> x0, blocking collectives: 120 us -> none  [shards(): lax.psum((jnp.sum(resid * applied), jnp.sum(applied * applied)), ('st', '...]
    pallas_call x0 -> x1, Pallas kernels: none -> 80.9 us  [shards(): pl.pallas_call(functools.partial(kernel, st_n, tm_n), out_shape=(jax.Shap...]
    dot_general x5 -> x0, matrix products: 63.5 us -> none  [the longest x2 36.2 us: shards(): jnp.einsum('bkij,bkjt->bit', kernel_tiles, grouped, precision=HIGHEST_PREC)]
    ppermute x10 -> x0, waiting for transfers between devices: 28.3 us -> none  [the longest x5 15.1 us: with_halo(): lax.ppermute(lax.slice_in_dim(block, 0, width, axis=dim), axis, backward)]
    gather x3 -> x0, local copies, waits for them, and re-layouts: 24.1 us -> none  [the longest x2 23.5 us: shards(): grouped = padded.reshape(span, BS, tm_width)[local_ids]]
    ppermute x10 -> x0, starting transfers between devices: 20 us -> none  [the longest x5 13.2 us: with_halo(): lax.ppermute(lax.slice_in_dim(block, block.shape[dim] - width, None, axis...]
    concatenate x2 -> x0, other arithmetic: 8.67 us -> none  [with_halo(): block = jnp.concatenate([low, block, high], axis=dim)]
    slice x9 -> x0, local copies, waits for them, and re-layouts: 4.98 us -> none  [the longest x4 4.18 us: with_halo(): lax.slice_in_dim(block, block.shape[dim] - width, None, axis=dim)]
  transfers between devices with their start and end apart: 10 -> 0, of which waited for: 7 -> 0; matrix products, arithmetic and copies ran while one was open for 4% -> 0% of each run, Pallas kernels for 0% -> 0%
where the time goes in v1:
time: 90.2 us; the launch traced here: 89.9 us
  Pallas kernels  80.9 us (90%)
  local copies, waits for them, and re-layouts  8.3 us (9%)
    pallas_call x1, Pallas kernels, shards(): pl.pallas_call(functools.partial(kernel, st_n, tm_n), out_shape=(jax.Shap...  80.9 us
    unnamed x5, local copies, waits for them, and re-layouts  5.69 us

profile of v1, /device:TPU:0, one launch (start us, length us, event | category | flops | bytes accessed | tf_op | source)
XLA Modules:
  0.0 89.9 jit_solution(4417600306218219962)
XLA Ops:
  0.6 1.3 %reshape.14.pxy = f32[2,4,128]{2,1,0:T(4,128)} reshape(f32[2,512]{1,0:T(2,128)} %param.8) | data formatting | bytes 8192 | tf_op jit(solution)/shard_map/reshape | solution.py:525
  1.9 0.7 reshape.13
  2.6 0.6 copy.12
  3.2 1.5 %copy.10.site_blocks = s32[512,4]{1,0:T(8,128)} copy(s32[512,4]{0,1:T(4,128)} %param.11) | data formatting | bytes 16384 | tf_op args[5]
  4.8 80.9 %shard_map.77 = (f32[1024,512]{1,0:T(8,128)}, f32[512,512]{1,0:T(8,128)}) custom-call(f32[1024,512]{1,0:T(8,128)} %obs.1, f32[2,2,4,128]{3,2,1,0:T(4,128)} %bitcast.4, f32[2,4,128]{2,1,0:T(4,128)} %reshape.14.pxy, f32[16,128]{1,0:T(8,128)} %bitcast.5, s32[8,9]{1,0:T(8,128)} %pattern.1, s32[512,4]{1,0:T(8,128)} %copy.10.site_blocks), custom_call_target="tpu_custom_call" | custom-call | tf_op jit(solution)/shard_map/pallas_call | solution.py:529
  85.7 0.0 copy-start
  85.7 3.2 %copy.15 = f32[1024,512]{1,0:T(8,128)} copy(f32[1024,512]{1,0:T(8,128)} %get-tuple-element.4) | data formatting | bytes 4194304
  88.9 0.0 copy-done
  88.9 1.0 %copy.16 = f32[512,512]{1,0:T(8,128)} copy(f32[512,512]{1,0:T(8,128)S(1)} %copy-done) | data formatting | bytes 2097152
Async XLA Ops:
  85.7 3.2 %copy-start = (f32[512,512]{1,0:T(8,128)S(1)}, f32[512,512]{1,0:T(8,128)}, u32[]{:S(2)}) copy-start(f32[512,512]{1,0:T(8,128)} %get-tuple-element.5) | copy-start | bytes 3145732

commit v2 on v1

v2 whole, which is shorter than its diff:
```python
import functools
import math

import jax
import jax.numpy as jnp
from jax import lax
from jax.experimental import pallas as pl
from jax.experimental.pallas import tpu as pltpu
from jax.sharding import PartitionSpec as P

BS = 128
REACH = 4
TREACH = 16
NNZ = 9
NNB = 4
NT = 2048
ITERS = 2
NUGGET = 1.0
MESH = pl.DeviceIdType.MESH
F32 = jnp.float32
BF16 = jnp.bfloat16


def wendland(radius, four, five):
    remain = jnp.maximum(1.0 - radius, 0.0)
    square = remain * remain
    return square * square * (five - four * remain)


def split(x):
    hi = x.astype(BF16)
    return hi, (x - hi.astype(F32)).astype(BF16)


def dot(a, b):
    return jnp.dot(a, b, preferred_element_type=F32)


def dot3(ah, al, bh, bl):
    return dot(ah, bh) + dot(ah, bl) + dot(al, bh)


def column(row):
    return jnp.transpose(jnp.broadcast_to(row, (BS, BS)))


def fold(x):
    rows, cols = x.shape
    x = jnp.sum(x.reshape(rows // 8, 8, cols), axis=0)
    total = x[:, :BS]
    for start in range(BS, cols, BS):
        total = total + x[:, start : start + BS]
    return total


def kernel(
    st_n,
    tm_n,
    obs,
    sxy,
    pxy,
    times,
    pattern,
    site_blocks,
    sol,
    pred,
    near,
    nx,
    ny,
    edge_out,
    edge_in,
    edge_parts,
    band_hi,
    band_lo,
    edge_band,
    halo,
    pad_hi,
    pad_lo,
    k_hi,
    k_lo,
    w_hi,
    w_lo,
    field,
    resid,
    pred_next,
    sums_tm,
    sums_st,
    xy_send,
    xy_recv,
    edge_send,
    edge_recv,
    halo_send,
    halo_recv,
    tm_send,
    tm_recv,
    st_send,
    st_recv,
):
    rows, width = obs.shape
    blocks = pattern.shape[0]
    sites = site_blocks.shape[1]
    margin = REACH * BS
    span = blocks + 2 * REACH
    chunk = 2 * BS
    pairs = blocks // 2
    lanes = width // BS
    st = lax.axis_index("st")
    tm = lax.axis_index("tm")
    has_low, has_high = st > 0, st < st_n - 1
    has_left, has_right = tm > 0, tm < tm_n - 1

    @pl.when(st == 0)
    def _():
        near[0] = jnp.zeros_like(near[0])
        for it in range(ITERS):
            halo[it, :margin] = jnp.zeros((margin, width), F32)

    @pl.when(st == st_n - 1)
    def _():
        near[1] = jnp.zeros_like(near[1])
        for it in range(ITERS):
            halo[it, margin:] = jnp.zeros((margin, width), F32)

    edge_in[...] = jnp.zeros_like(edge_in)

    barrier = pltpu.get_barrier_semaphore()
    for d in range(1, st_n):
        pl.semaphore_signal(barrier, inc=1, device_id={"st": (st + d) % st_n}, device_id_type=MESH)
    for d in range(1, tm_n):
        pl.semaphore_signal(barrier, inc=1, device_id={"tm": (tm + d) % tm_n}, device_id_type=MESH)
    for i in (st_n - 1, 1):
        for j in (tm_n - 1, 1):
            pl.semaphore_signal(
                barrier,
                inc=1,
                device_id={"st": (st + i) % st_n, "tm": (tm + j) % tm_n},
                device_id_type=MESH,
            )

    def shift(src, dst, send, recv, axis, pos, count, step):
        return pltpu.make_async_remote_copy(
            src_ref=src,
            dst_ref=dst,
            send_sem=send,
            recv_sem=recv,
            device_id={axis: (pos + step + count) % count},
            device_id_type=MESH,
        )

    def xy_copy(up):
        if up:
            return shift(sxy.at[:, pl.ds(rows - margin, margin)], near.at[0], xy_send.at[0],
                         xy_recv.at[0], "st", st, st_n, 1)
        return shift(sxy.at[:, pl.ds(0, margin)], near.at[1], xy_send.at[1], xy_recv.at[1],
                     "st", st, st_n, -1)

    def edge_copy(it, k, side):
        begin, count = ((0, rows), (rows - margin, margin), (0, margin))[side]
        target = (margin, 0, margin + rows)[side]
        to_tm = (tm + (1 if k else tm_n - 1)) % tm_n
        to_st = (st + (0, 1, st_n - 1)[side]) % st_n
        return pltpu.make_async_remote_copy(
            src_ref=edge_out.at[it, k, :, pl.ds(begin, count)],
            dst_ref=edge_in.at[it, k, :, pl.ds(target, count)],
            send_sem=edge_send.at[it, k, side],
            recv_sem=edge_recv.at[it, k, side],
            device_id={"st": to_st, "tm": to_tm},
            device_id_type=MESH,
        )

    send_tm = (has_left, has_right)
    recv_tm = (has_right, has_left)
    always = st >= 0
    send_st = (always, has_high, has_low)
    recv_st = (always, has_low, has_high)

    halves = margin // chunk

    def halo_copy(it, up, part):
        k = 1 if up else 0
        source = rows - margin + part * chunk if up else part * chunk
        target = part * chunk if up else margin + part * chunk
        origin = obs if it == 0 else field
        return shift(
            origin.at[pl.ds(source, chunk)],
            halo.at[it, pl.ds(target, chunk)],
            halo_send.at[it, k, part],
            halo_recv.at[it, k, part],
            "st", st, st_n, 1 if up else -1,
        )

    def start_halo(it, up, part):
        @pl.when(has_high if up else has_low)
        def _():
            halo_copy(it, up, part).start()

    def wait_halo(it, up, part):
        @pl.when(has_low if up else has_high)
        def _():
            halo_copy(it, up, part).wait_recv()

    def take_edges(source, it):
        for b in range(blocks):
            here = slice(b * BS, (b + 1) * BS)
            edge_out[it, 0, :, here] = jnp.transpose(source[here, :BS])[:TREACH]
            edge_out[it, 1, :, here] = jnp.transpose(source[here, width - BS :])[BS - TREACH :]

    def each_edge(send, action):
        tm_ok, st_ok = (send_tm, send_st) if send else (recv_tm, recv_st)
        for side in range(3):
            for k in range(2):
                @pl.when(jnp.logical_and(tm_ok[k], st_ok[side]))
                def _(k=k, side=side):
                    action(k, side)

    def start_edges(it):
        each_edge(True, lambda k, side: edge_copy(it, k, side).start())

    def finish_edges(it):
        each_edge(False, lambda k, side: edge_copy(it, k, side).wait_recv())

    def stack_edges(left, right):
        for k, value in ((1, left), (0, right)):
            hi, lo = split(value)
            edge_parts[k] = jnp.concatenate([hi, hi, lo], axis=0)

    def mix_rows(it, begin, value):
        hi, lo = split(value)
        mixed = dot3(hi, lo, band_hi[...], band_lo[...])
        sides = []
        for k in (1, 0):
            sides.append(lax.dot_general(
                edge_parts[k, :, begin : begin + chunk],
                edge_band[k],
                (((0,), (0,)), ((), ())),
                preferred_element_type=F32,
            ))
        mixed = jnp.concatenate(
            [mixed[:, :BS] + sides[0], mixed[:, BS : width - BS], mixed[:, width - BS :] + sides[1]],
            axis=1,
        )
        here = pl.ds(begin, chunk)
        pad_hi[it, here, :], pad_lo[it, here, :] = split(mixed)

    def mix_halo(it, step):
        for part in range(halves):
            for up in (True, False):
                wait_halo(it, up, part)
                first = part * chunk if up else margin + part * chunk
                here = pl.ds(first, chunk)
                value = halo[0, here, :]
                if it:
                    value = value - step * halo[1, here, :]
                mix_rows(it, first if up else first + rows, value)

    half = min(width, 256)

    def apply_part(it, p, begin, end, col):
        here = slice(p * chunk, (p + 1) * chunk)
        cols = slice((begin - 2 * p) * BS, (end - 2 * p) * BS)
        ins = slice(begin * BS, end * BS)
        return dot3(
            k_hi[here, cols], k_lo[here, cols], pad_hi[it, ins, col], pad_lo[it, ins, col]
        )

    fields = (field, sol)

    def apply_own(it):
        @pl.loop(0, width // half)
        def _(n):
            col = pl.ds(pl.multiple_of(n * half, half), half)
            for p in range(pairs):
                begin = max(2 * p, REACH)
                end = min(2 * p + 2 + 2 * REACH, REACH + blocks)
                fields[it][p * chunk : (p + 1) * chunk, col] = apply_part(it, p, begin, end, col)

    def apply_halo(it, p, source):
        begin = max(2 * p, REACH)
        end = min(2 * p + 2 + 2 * REACH, REACH + blocks)
        here = slice(p * chunk, (p + 1) * chunk)
        inner = jnp.zeros((8, BS), F32)
        energy = jnp.zeros((8, BS), F32)
        for n in range(width // half):
            col = slice(n * half, (n + 1) * half)
            value = fields[it][here, col]
            if 2 * p < begin:
                value = value + apply_part(it, p, 2 * p, begin, col)
            if end < 2 * p + 2 + 2 * REACH:
                value = value + apply_part(it, p, end, 2 * p + 2 + 2 * REACH, col)
            old = source[here, col]
            value = value + NUGGET * old
            fields[it][here, col] = value
            inner = inner + fold(old * value)
            energy = energy + fold(value * value)
        return inner, energy

    def finish_apply(it, source):
        inner = jnp.zeros((8, BS), F32)
        energy = jnp.zeros((8, BS), F32)
        for p in range(pairs):
            one, two = apply_halo(it, p, source)
            inner, energy = inner + one, energy + two
            if it == 0:
                if p < halves:
                    start_halo(1, False, p)
                if p >= pairs - halves:
                    start_halo(1, True, p - (pairs - halves))
        sums_tm[it, 0, :8] = inner
        sums_tm[it, 0, 8:] = energy

    def sum_copy(it, axis, d):
        if axis == "tm":
            return shift(sums_tm.at[it, 0], sums_tm.at[it, d], tm_send.at[it, d - 1],
                         tm_recv.at[it, d - 1], "tm", tm, tm_n, d)
        return shift(sums_st.at[it, 0], sums_st.at[it, d], st_send.at[it, d - 1],
                     st_recv.at[it, d - 1], "st", st, st_n, d)

    def start_sum(it, axis):
        for d in range(1, tm_n if axis == "tm" else st_n):
            sum_copy(it, axis, d).start()

    def finish_sum(it, axis):
        count, pos, buf = (tm_n, tm, sums_tm) if axis == "tm" else (st_n, st, sums_st)
        for d in range(1, count):
            sum_copy(it, axis, d).wait_recv()
        total = buf[it, pos % count]
        for j in range(1, count):
            total = total + buf[it, (pos - j + count) % count]
        return total

    def step_of(it):
        total = finish_sum(it, "st")
        inner = jnp.sum(jnp.sum(total[:8], axis=0, keepdims=True), axis=1, keepdims=True)
        energy = jnp.sum(jnp.sum(total[8:], axis=0, keepdims=True), axis=1, keepdims=True)
        return inner / (energy + 1e-06)

    take_edges(obs, 0)
    pl.semaphore_wait(barrier, st_n - 1 + tm_n - 1 + 4)
    start_edges(0)

    for part in range(halves):
        start_halo(0, False, part)
        start_halo(0, True, part)

    @pl.when(has_high)
    def _():
        xy_copy(True).start()

    @pl.when(has_low)
    def _():
        xy_copy(False).start()

    def time_row(i):
        count = times.shape[0]
        return times[pl.ds((tm * lanes + i + count) % count, 1), :]

    def time_tile(i, j):
        apart = jnp.abs(column(time_row(i)) - time_row(j))
        return wendland(apart * (NT / TREACH), 10.0 / math.sqrt(TREACH), 12.5 / math.sqrt(TREACH))

    for i in range(lanes):
        for j in range(lanes):
            a = slice(i * BS, (i + 1) * BS)
            b = slice(j * BS, (j + 1) * BS)
            if abs(i - j) <= 1:
                band_hi[a, b], band_lo[a, b] = split(time_tile(i, j))
            else:
                band_hi[a, b] = jnp.zeros((BS, BS), BF16)
                band_lo[a, b] = jnp.zeros((BS, BS), BF16)
    for k, tile in (
        (1, time_tile(-1, 0)[BS - TREACH :]),
        (0, time_tile(lanes, lanes - 1)[:TREACH]),
    ):
        hi, lo = split(tile)
        edge_band[k] = jnp.concatenate([hi, lo, hi], axis=0)

    finish_edges(0)
    stack_edges(edge_in[0, 1], edge_in[0, 0])
    for c in range(rows // chunk):
        mix_rows(0, margin + c * chunk, obs[c * chunk : (c + 1) * chunk, :])

    @pl.when(has_low)
    def _():
        xy_copy(True).wait_recv()

    @pl.when(has_high)
    def _():
        xy_copy(False).wait_recv()

    third = 1.0 / (0.75 * REACH)
    for c, out in enumerate((nx, ny)):
        for b in range(REACH):
            lane = slice(b * BS, (b + 1) * BS)
            out[b : b + 1, :] = near[0, c : c + 1, lane] * third
            high = REACH + blocks + b
            out[high : high + 1, :] = near[1, c : c + 1, lane] * third
        for b in range(blocks):
            out[REACH + b : REACH + b + 1, :] = sxy[c : c + 1, b * BS : (b + 1) * BS] * third

    lane_ids = lax.broadcasted_iota(jnp.int32, (BS, BS), 1)
    ids = pattern[...]
    k_counts = jnp.zeros((blocks, BS), F32)
    for s in range(NNZ):
        hit = ids[:, s : s + 1] == lane_ids[:blocks] + (st * blocks - REACH)
        k_counts = k_counts + hit.astype(F32)

    def weight(xcol, ycol, block, four, five):
        dx = xcol - nx[pl.ds(block, 1), :]
        dy = ycol - ny[pl.ds(block, 1), :]
        square = dx * dx + dy * dy + 0.0001 * third * third
        return wendland(square * lax.rsqrt(square), four, five)

    for p in range(pairs):
        for q in range(2):
            b = 2 * p + q
            here = slice(b * BS, (b + 1) * BS)
            xcol = column(nx[REACH + b : REACH + b + 1, :])
            ycol = column(ny[REACH + b : REACH + b + 1, :])
            gap = (2 * REACH + 1 if q == 0 else 0) * BS
            k_hi[here, gap : gap + BS] = jnp.zeros((BS, BS), BF16)
            k_lo[here, gap : gap + BS] = jnp.zeros((BS, BS), BF16)
            for k in range(2 * REACH + 1):
                count = jnp.broadcast_to(k_counts[b : b + 1, b + k : b + k + 1], (1, BS))
                unit = 2.5 / math.sqrt(NNZ * BS)
                tile = weight(xcol, ycol, b + k, count * (4.0 * unit), count * (5.0 * unit))
                cols = slice((q + k) * BS, (q + k + 1) * BS)
                k_hi[here, cols], k_lo[here, cols] = split(tile)

    apply_own(0)
    mix_halo(0, None)
    finish_apply(0, obs)
    start_sum(0, "tm")
    take_edges(field, 1)
    start_edges(1)
    sums_st[0, 0] = finish_sum(0, "tm")
    start_sum(0, "st")

    per_group = BS // (sites // blocks)
    wide = w_hi.shape[1] // BS
    site_chunks = sites // BS
    chunks_per = chunk // BS

    def site_tiles(h):
        here = slice(h * BS, (h + 1) * BS)
        base = (h // chunks_per) * chunks_per * per_group
        xcol = column(pxy[0:1, here] * third)
        ycol = column(pxy[1:2, here] * third)
        counts = jnp.zeros((BS, BS), F32)
        for s in range(NNB):
            listed = column((site_blocks[s : s + 1, here] - st * blocks).astype(F32))
            hit = listed == (lane_ids + (base - REACH)).astype(F32)
            counts = counts + hit.astype(F32)
        first = h * per_group - base
        for k in range(wide):
            cols = slice(k * BS, (k + 1) * BS)
            if first <= k < first + per_group + 2 * REACH:
                count = counts[:, k : k + 1]
                unit = 2.5 / math.sqrt(NNB * BS)
                tile = weight(xcol, ycol, base + k, count * (4.0 * unit), count * (5.0 * unit))
                w_hi[here, cols], w_lo[here, cols] = split(tile)
            else:
                w_hi[here, cols] = jnp.zeros((BS, BS), BF16)
                w_lo[here, cols] = jnp.zeros((BS, BS), BF16)

    for h in range(site_chunks):
        site_tiles(h)

    finish_edges(1)
    step0 = step_of(0)
    stack_edges(
        edge_in[0, 1] - step0 * edge_in[1, 1],
        edge_in[0, 0] - step0 * edge_in[1, 0],
    )
    for c in range(rows // chunk):
        here = slice(c * chunk, (c + 1) * chunk)
        value = obs[here, :] - step0 * field[here, :]
        resid[here, :] = value
        mix_rows(1, margin + c * chunk, value)

    def predict(it, out):
        @pl.loop(0, width // half)
        def _(n):
            col = pl.ds(pl.multiple_of(n * half, half), half)
            for g in range(sites // chunk):
                here = slice(g * chunk, (g + 1) * chunk)
                base = g * chunks_per * per_group * BS
                ins = slice(base, base + wide * BS)
                out[here, col] = dot3(
                    w_hi[here, :], w_lo[here, :], pad_hi[it, ins, col], pad_lo[it, ins, col]
                )

    apply_own(1)
    predict(0, pred)
    mix_halo(1, step0)
    finish_apply(1, resid)
    start_sum(1, "tm")
    sums_st[1, 0] = finish_sum(1, "tm")
    start_sum(1, "st")
    predict(1, pred_next)
    step1 = step_of(1)
    for c in range(rows // chunk):
        here = slice(c * chunk, (c + 1) * chunk)
        sol[here, :] = step0 * obs[here, :] + step1 * resid[here, :]
    for c in range(sites // chunk):
        here = slice(c * chunk, (c + 1) * chunk)
        pred[here, :] = step0 * pred[here, :] + step1 * pred_next[here, :]

    for up in (True, False):
        @pl.when(has_high if up else has_low)
        def _(up=up):
            xy_copy(up).wait_send()
            for part in range(halves):
                for it in range(ITERS):
                    halo_copy(it, up, part).wait_send()

    for it in range(ITERS):
        each_edge(True, lambda k, side: edge_copy(it, k, side).wait_send())

    for it in range(ITERS):
        for axis, count in (("tm", tm_n), ("st", st_n)):
            for d in range(1, count):
                sum_copy(it, axis, d).wait_send()


def shards(st_n, tm_n, observed, station_xy, site_xy, time_points, pattern, site_blocks):
    rows, width = observed.shape
    blocks = pattern.shape[0]
    sites = site_blocks.shape[0]
    padded = rows + 2 * REACH * BS
    per_group = BS // (sites // blocks)
    wide = (2 * per_group + 2 * REACH) * BS
    halves = REACH // 2
    times = time_points.reshape(-1, BS)
    vmem = pl.BlockSpec(memory_space=pltpu.VMEM)
    dma = pltpu.SemaphoreType.DMA
    return pl.pallas_call(
        functools.partial(kernel, st_n, tm_n),
        out_shape=(
            jax.ShapeDtypeStruct((rows, width), F32),
            jax.ShapeDtypeStruct((sites, width), F32),
        ),
        in_specs=[vmem] * 6,
        out_specs=(vmem, vmem),
        scratch_shapes=[
            pltpu.VMEM((2, 2, REACH * BS), F32),
            pltpu.VMEM((blocks + 2 * REACH, BS), F32),
            pltpu.VMEM((blocks + 2 * REACH, BS), F32),
            pltpu.VMEM((ITERS, 2, TREACH, rows), F32),
            pltpu.VMEM((ITERS, 2, TREACH, padded), F32),
            pltpu.VMEM((2, 3 * TREACH, padded), BF16),
            pltpu.VMEM((width, width), BF16),
            pltpu.VMEM((width, width), BF16),
            pltpu.VMEM((2, 3 * TREACH, BS), BF16),
            pltpu.VMEM((ITERS, 2 * REACH * BS, width), F32),
            pltpu.VMEM((ITERS, padded, width), BF16),
            pltpu.VMEM((ITERS, padded, width), BF16),
            pltpu.VMEM((rows, (2 + 2 * REACH) * BS), BF16),
            pltpu.VMEM((rows, (2 + 2 * REACH) * BS), BF16),
            pltpu.VMEM((sites, wide), BF16),
            pltpu.VMEM((sites, wide), BF16),
            pltpu.VMEM((rows, width), F32),
            pltpu.VMEM((rows, width), F32),
            pltpu.VMEM((sites, width), F32),
            pltpu.VMEM((ITERS, tm_n, 16, BS), F32),
            pltpu.VMEM((ITERS, st_n, 16, BS), F32),
            dma((2,)),
            dma((2,)),
            dma((ITERS, 2, 3)),
            dma((ITERS, 2, 3)),
            dma((ITERS, 2, halves)),
            dma((ITERS, 2, halves)),
            dma((ITERS, tm_n - 1)),
            dma((ITERS, tm_n - 1)),
            dma((ITERS, st_n - 1)),
            dma((ITERS, st_n - 1)),
        ],
        compiler_params=pltpu.CompilerParams(
            collective_id=0, has_side_effects=True, vmem_limit_bytes=60 * 1024 * 1024
        ),
    )(observed, station_xy, site_xy, times, pattern, site_blocks.T)


def solution(mesh):
    placed = (P("st", "tm"), P(None, "st"), P(None, "st"), P(), P("st", None), P("st", None))
    return jax.shard_map(
        functools.partial(shards, mesh.shape["st"], mesh.shape["tm"]),
        mesh=mesh,
        in_specs=placed,
        out_specs=(P("st", "tm"), P("st", "tm")),
        check_vma=False,
    )
```

time: 90.2 us -> 85.1 us (0.943)
  local copies, waits for them, and re-layouts: 8.3 us -> 4.14 us
    reshape x3 -> x0, local copies, waits for them, and re-layouts: 2.61 us -> none  [the longest x2 1.31 us: shards(): sxy = station_xy.reshape(2, groups, REACH, BS).transpose(1, 0, 2, 3)]
    unnamed x5 -> x4, local copies, waits for them, and re-layouts: 5.69 us -> 4.14 us
where the time goes in v2:
time: 85.1 us; the launch traced here: 85 us
  Pallas kernels  80.2 us (94%)
  local copies, waits for them, and re-layouts  4.14 us (5%)
    pallas_call x1, Pallas kernels, shards(): pl.pallas_call(functools.partial(kernel, st_n, tm_n), out_shape=(jax.Shap...  80.2 us
    unnamed x4, local copies, waits for them, and re-layouts  4.14 us

profile of v2, /device:TPU:0, one launch (start us, length us, event | category | flops | bytes accessed | tf_op | source)
XLA Modules:
  0.0 85.0 jit_solution(16115553052996346800)
XLA Ops:
  0.6 80.2 %shard_map.77 = (f32[1024,512]{1,0:T(8,128)}, f32[512,512]{1,0:T(8,128)}) custom-call(f32[1024,512]{1,0:T(8,128)} %obs.1, f32[2,1024]{1,0:T(2,128)} %sxy.1, f32[2,512]{1,0:T(2,128)} %pxy.1, f32[16,128]{1,0:T(8,128)} %bitcast.2, s32[8,9]{1,0:T(8,128)} %pattern.1, s32[4,512]{1,0:T(4,128)} %bitcast.3), custom_call_target="tpu_custom_call" | custom-call | tf_op jit(solution)/shard_map/pallas_call | solution.py:536
  80.8 0.0 copy-start
  80.8 3.2 %copy.10 = f32[1024,512]{1,0:T(8,128)} copy(f32[1024,512]{1,0:T(8,128)} %get-tuple-element.4) | data formatting | bytes 4194304
  84.0 0.0 copy-done
  84.0 1.0 %copy.11 = f32[512,512]{1,0:T(8,128)} copy(f32[512,512]{1,0:T(8,128)S(1)} %copy-done) | data formatting | bytes 2097152
Async XLA Ops:
  80.8 3.2 %copy-start = (f32[512,512]{1,0:T(8,128)S(1)}, f32[512,512]{1,0:T(8,128)}, u32[]{:S(2)}) copy-start(f32[512,512]{1,0:T(8,128)} %get-tuple-element.5) | copy-start | bytes 3145732
